TPU v7x, 32 devices: a whole 2x2x4 slice. The times are simulated.
32 devices in a mesh: member: 8 (over z, x), space: 4 (over y, core).
Axes of the slice: x: 2, y: 2, z: 4, core: 2. Of those that a mesh axis runs over, the one named last changes fastest.
Arguments:
- alpha: float32 [16, 16, 32, 1280], P('member', None, 'space'), may hold values from -6 to 6
- perturb: bfloat16 [4, 16, 16, 32, 1280], P(None, 'member', None, 'space'), may hold values from -1.5 to 1.5
- kappa: float32 [32, 1280], P('space'), may hold values from 0.1 to 0.24
- land: int32 [32, 1280], P('space'), may hold values 0 or 1
- obs_weight: float32 [4, 16, 32, 1280], P(None, 'member', 'space'), may hold values from 0.2 to 5
- innovation: float32 [4, 16, 32, 1280], P(None, 'member', 'space'), may hold values from -6 to 6
Outputs:
- gradient: float32 [16, 16, 32, 1280], P('member', None, 'space')
- weighted_misfit: float32 [4, 16, 32, 1280], P(None, 'member', 'space')
All inputs are finite; a program needn't handle non-finite values. No bound on the sum of `land` on one device may be relied on, other than what follows from the above.
Results may differ from a plain program's by a relative error of at most 0.0003.
Values sent between devices are 32-bit elements; how exact they have to be, the bound alone decides.
No kernel may reach another device: no remote copies, remote signals or barrier semaphores. Data moves between devices by JAX's collectives and lax.ppermute only.
A program may use at most 64 MiB of HBM per device.

v0:
```python
import jax
import jax.numpy as jnp
from jax import lax
from jax.sharding import PartitionSpec as P

STEPS = 4


def extended_2(cells, sides, width):
    for axis, dim in sides:
        count = lax.axis_size(axis)
        ends = count - 1
        head = lax.slice_in_dim(cells, 0, width, axis=dim)
        tail = lax.slice_in_dim(cells, cells.shape[dim] - width, cells.shape[dim], axis=dim)
        cells = jnp.concatenate(
            [
                lax.ppermute(tail, axis, [(i, (i + 1) % count) for i in range(ends)]),
                cells,
                lax.ppermute(head, axis, [((i + 1) % count, i) for i in range(ends)]),
            ],
            axis=dim,
        )
    return cells


def smooth_step(padded, coef_east, coef_west, coef_north, coef_south):
    middle = padded[:, :, 1:-1, :]
    return (
        middle
        + coef_east * (jnp.roll(middle, -1, axis=-1) - middle)
        + coef_west * (jnp.roll(middle, 1, axis=-1) - middle)
        + coef_north * (padded[:, :, 2:, :] - middle)
        + coef_south * (padded[:, :, :-2, :] - middle)
    )


def body(alpha, perturb, kappa, land, obs_weight, innovation):
    tile_rows = alpha.shape[2]
    extended = extended_2(kappa, (("space", 0),), STEPS + 1)
    inner = extended[1:-1]
    coef_north = 0.5 * (inner + extended[2:])
    coef_south = 0.5 * (inner + extended[:-2])
    coef_east = 0.5 * (inner + jnp.roll(inner, -1, axis=1))
    coef_west = 0.5 * (inner + jnp.roll(inner, 1, axis=1))

    def diffuse(field):
        current = field
        for sweep in range(STEPS):
            padded = extended_2(current, (("space", 2),), 1)
            current = smooth_step(
                padded,
                coef_east[STEPS : STEPS + tile_rows],
                coef_west[STEPS : STEPS + tile_rows],
                coef_north[STEPS : STEPS + tile_rows],
                coef_south[STEPS : STEPS + tile_rows],
            )
        return current

    sea = land.astype(jnp.float32)
    local = diffuse(alpha) * sea
    partial_sum = jnp.sum(perturb * local[None], axis=1)
    total = lax.psum(partial_sum, "member")
    weight_all, innov_all = (
        lax.all_gather(obs_weight, "member", axis=1, tiled=True),
        lax.all_gather(innovation, "member", axis=1, tiled=True),
    )
    whole_misfit = weight_all * (total - innov_all)
    own_width = obs_weight.shape[1]
    weighted_misfit = lax.dynamic_slice_in_dim(
        whole_misfit, lax.axis_index("member") * own_width, own_width, 1
    )
    back = jnp.sum(perturb * whole_misfit[:, None], axis=0)
    gradient = diffuse(back * sea) + alpha
    return (gradient, weighted_misfit)


def solution(mesh):
    placed = (
        P("member", None, "space", None),
        P(None, "member", None, "space", None),
        P("space", None),
        P("space", None),
        P(None, "member", "space", None),
        P(None, "member", "space", None),
    )
    return jax.shard_map(
        body,
        mesh=mesh,
        in_specs=placed,
        out_specs=(P("member", None, "space", None), P(None, "member", "space", None)),
        check_vma=False,
    )
```

profile of v0, /device:TPU:1, one launch (start us, length us, event | category | flops | bytes accessed | tf_op | source)
XLA Modules:
  0.0 342.5 jit_solution(4764403704498449764)
XLA Ops:
  8.1 4.5 %collective-permute-start = (f32[5,1280]{1,0:T(8,128)S(1)}, f32[5,1280]{1,0:T(8,128)S(1)}, u32[]{:S(2)}, u32[]{:S(2)}) collective-permute-start(f32[5,1280]{1,0:T(8,128)S(1)} %get-tuple-element.61), channel_id=1, source_target_pairs={{0,1},{1,2},{2,3},{4,5},{5,6},{6,7},{8,9},{9,10},{10,11},{12,13},{... | collective-permute-start | bytes 76808 | tf_op jit(solution)/shard_map/ppermute | solution.py:17
  12.6 1.9 collective-permute-start.1
  14.6 2.1 fusion.113
  16.7 1.9 collective-permute-start.2
  18.7 3.8 %collective-permute-start.3 = (f32[2,16,1,1280]{3,1,2,0:T(8,128)S(1)}, f32[2,16,1,1280]{3,1,2,0:T(8,128)S(1)}, u32[]{:S(2)}, u32[]{:S(2)}) collective-permute-start(f32[2,16,1,1280]{3,1,2,0:T(8,128)S(1)} %copy.57), channel_id=1, source_target_pairs={{0,1},{1,2},{2,3},{4,5},{5,6},{6,7},{8,9},{9,10},{10,11},{12,13},{... | collective-permute-start | bytes 491528 | tf_op jit(solution)/shard_map/ppermute | solution.py:17
  26.5 1.9 collective-permute-start.4
  28.5 4.4 %collective-permute-start.5 = (f32[2,16,1,1280]{3,1,2,0:T(8,128)S(1)}, f32[2,16,1,1280]{3,1,2,0:T(8,128)S(1)}, u32[]{:S(2)}, u32[]{:S(2)}) collective-permute-start(f32[2,16,1,1280]{3,1,2,0:T(8,128)S(1)} %copy.30), channel_id=1, source_target_pairs={{0,1},{1,2},{2,3},{4,5},{5,6},{6,7},{8,9},{9,10},{10,11},{12,13},{... | collective-permute-start | bytes 491528 | tf_op jit(solution)/shard_map/ppermute | solution.py:17
  37.0 1.9 collective-permute-start.6
  38.9 4.4 %collective-permute-start.7 = (f32[2,16,1,1280]{3,1,2,0:T(8,128)S(1)}, f32[2,16,1,1280]{3,1,2,0:T(8,128)S(1)}, u32[]{:S(2)}, u32[]{:S(2)}) collective-permute-start(f32[2,16,1,1280]{3,1,2,0:T(8,128)S(1)} %copy.34), channel_id=1, source_target_pairs={{0,1},{1,2},{2,3},{4,5},{5,6},{6,7},{8,9},{9,10},{10,11},{12,13},{... | collective-permute-start | bytes 491528 | tf_op jit(solution)/shard_map/ppermute | solution.py:17
  47.4 1.9 collective-permute-start.8
  49.4 4.4 %collective-permute-start.9 = (f32[2,16,1,1280]{3,1,2,0:T(8,128)S(1)}, f32[2,16,1,1280]{3,1,2,0:T(8,128)S(1)}, u32[]{:S(2)}, u32[]{:S(2)}) collective-permute-start(f32[2,16,1,1280]{3,1,2,0:T(8,128)S(1)} %copy.38), channel_id=1, source_target_pairs={{0,1},{1,2},{2,3},{4,5},{5,6},{6,7},{8,9},{9,10},{10,11},{12,13},{... | collective-permute-start | bytes 491528 | tf_op jit(solution)/shard_map/ppermute | solution.py:17
  57.9 2.1 fusion
  61.6 115.5 %all-reduce.2.cloned.1.call-done = f32[4,16,8,1280]{3,2,1,0:T(8,128)} async-done(((f32[4,16,8,1280]{3,2,1,0:T(8,128)}), f32[4,16,8,1280]{3,2,1,0:T(8,128)}) %all-reduce.2.cloned.1.call-update) | async-done | bytes 2621456 | tf_op jit(solution)/shard_map/psum | solution.py:62
  177.0 55.2 %all-gather.3.cloned.1.call-done = f32[4,16,8,1280]{3,2,1,0:T(8,128)} async-done(((f32[4,2,8,1280]{3,2,1,0:T(8,128)}), f32[4,16,8,1280]{3,2,1,0:T(8,128)}) %all-gather.3.cloned.1.call-update) | async-done | bytes 2621456 | tf_op jit(solution)/shard_map/all_gather | solution.py:64
  232.2 55.2 %all-gather.5.cloned.1.call-done = f32[4,16,8,1280]{3,2,1,0:T(8,128)} async-done(((f32[4,2,8,1280]{3,2,1,0:T(8,128)}), f32[4,16,8,1280]{3,2,1,0:T(8,128)}) %all-gather.5.cloned.1.call-update) | async-done | bytes 2621456 | tf_op jit(solution)/shard_map/all_gather | solution.py:65
  287.5 3.9 %subtract_multiply_fusion = f32[4,16,8,1280]{3,2,1,0:T(8,128)S(1)} fusion(f32[4,16,8,1280]{3,2,1,0:T(8,128)} %all-gather.3.cloned.1.call-done, f32[4,16,8,1280]{3,2,1,0:T(8,128)} %all-reduce.2.cloned.1.call-done, f32[4,16,8,1280]{3,2,1,0:T(8,128)} %all-gather.5.cloned.1.call-done), kind=kLoop, calls=%fused_computation.4 | loop fusion | flops 1310720 | bytes 10485760 | tf_op jit(solution)/shard_map/mul | solution.py:67
  292.8 4.2 %collective-permute-start.10 = (f32[2,16,1,1280]{3,1,2,0:T(8,128)S(1)}, f32[2,16,1,1280]{3,1,2,0:T(8,128)S(1)}, u32[]{:S(2)}, u32[]{:S(2)}) collective-permute-start(f32[2,16,1,1280]{3,1,2,0:T(8,128)S(1)} %copy.40), channel_id=1, source_target_pairs={{1,0},{2,1},{3,2},{5,4},{6,5},{7,6},{9,8},{10,9},{11,10},{13,12},{... | collective-permute-start | bytes 491528 | tf_op jit(solution)/shard_map/ppermute | solution.py:19
  297.0 3.0 collective-permute-start.11
  304.1 1.9 collective-permute-start.12
  306.1 4.4 %collective-permute-start.13 = (f32[2,16,1,1280]{3,1,2,0:T(8,128)S(1)}, f32[2,16,1,1280]{3,1,2,0:T(8,128)S(1)}, u32[]{:S(2)}, u32[]{:S(2)}) collective-permute-start(f32[2,16,1,1280]{3,1,2,0:T(8,128)S(1)} %copy.46), channel_id=1, source_target_pairs={{0,1},{1,2},{2,3},{4,5},{5,6},{6,7},{8,9},{9,10},{10,11},{12,13},{... | collective-permute-start | bytes 491528 | tf_op jit(solution)/shard_map/ppermute | solution.py:17
  314.6 1.9 collective-permute-start.14
  316.5 4.4 %collective-permute-start.15 = (f32[2,16,1,1280]{3,1,2,0:T(8,128)S(1)}, f32[2,16,1,1280]{3,1,2,0:T(8,128)S(1)}, u32[]{:S(2)}, u32[]{:S(2)}) collective-permute-start(f32[2,16,1,1280]{3,1,2,0:T(8,128)S(1)} %copy.50), channel_id=1, source_target_pairs={{0,1},{1,2},{2,3},{4,5},{5,6},{6,7},{8,9},{9,10},{10,11},{12,13},{... | collective-permute-start | bytes 491528 | tf_op jit(solution)/shard_map/ppermute | solution.py:17
  327.0 4.4 %collective-permute-start.17 = (f32[2,16,1,1280]{3,1,2,0:T(8,128)S(1)}, f32[2,16,1,1280]{3,1,2,0:T(8,128)S(1)}, u32[]{:S(2)}, u32[]{:S(2)}) collective-permute-start(f32[2,16,1,1280]{3,1,2,0:T(8,128)S(1)} %copy.54), channel_id=1, source_target_pairs={{0,1},{1,2},{2,3},{4,5},{5,6},{6,7},{8,9},{9,10},{10,11},{12,13},{... | collective-permute-start | bytes 491528 | tf_op jit(solution)/shard_map/ppermute | solution.py:17
  333.8 2.2 fusion.5
  (106 shorter events, 36.7 us)
Async XLA Ops:
  7.2 15.3 %copy-start = (f32[2,16,8,1280]{3,2,1,0:T(8,128)S(1)}, f32[2,16,8,1280]{3,2,1,0:T(8,128)}, u32[]{:S(2)}) copy-start(f32[2,16,8,1280]{3,2,1,0:T(8,128)} %param.6) | copy-start | bytes 3932164
  7.2 169.9 %all-reduce.2.cloned.1.call-start = ((), (), s32[]{:S(2)}) async-start(), calls=%async_computation.1 | async-start | bytes 5242880 | tf_op jit(solution)/shard_map/psum | solution.py:62
  8.1 14.9 %collective-permute-start = (f32[5,1280]{1,0:T(8,128)S(1)}, f32[5,1280]{1,0:T(8,128)S(1)}, u32[]{:S(2)}, u32[]{:S(2)}) collective-permute-start(f32[5,1280]{1,0:T(8,128)S(1)} %get-tuple-element.61), channel_id=1, source_target_pairs={{0,1},{1,2},{2,3},{4,5},{5,6},{6,7},{8,9},{9,10},{10,11},{12,13},{... | collective-permute-start | bytes 76808 | tf_op jit(solution)/shard_map/ppermute | solution.py:17
  12.6 10.4 %collective-permute-start.1 = (f32[5,1280]{1,0:T(8,128)S(1)}, f32[5,1280]{1,0:T(8,128)S(1)}, u32[]{:S(2)}, u32[]{:S(2)}) collective-permute-start(f32[5,1280]{1,0:T(8,128)S(1)} %get-tuple-element.62), channel_id=1, source_target_pairs={{1,0},{2,1},{3,2},{5,4},{6,5},{7,6},{9,8},{10,9},{11,10},{13,12},{... | collective-permute-start | bytes 76808 | tf_op jit(solution)/shard_map/ppermute | solution.py:19
  16.7 6.6 %collective-permute-start.2 = (f32[2,16,1,1280]{3,1,2,0:T(8,128)S(1)}, f32[2,16,1,1280]{3,1,2,0:T(8,128)S(1)}, u32[]{:S(2)}, u32[]{:S(2)}) collective-permute-start(f32[2,16,1,1280]{3,1,2,0:T(8,128)S(1)} %copy.56), channel_id=1, source_target_pairs={{1,0},{2,1},{3,2},{5,4},{6,5},{7,6},{9,8},{10,9},{11,10},{13,12},{... | collective-permute-start | bytes 491528 | tf_op jit(solution)/shard_map/ppermute | solution.py:19
  18.6 4.3 %copy-start.4 = (s32[8,1280]{1,0:T(8,128)S(1)}, s32[8,1280]{1,0:T(8,128)}, u32[]{:S(2)}) copy-start(s32[8,1280]{1,0:T(8,128)} %param.9) | copy-start | bytes 122884
  18.6 4.4 %copy-start.3 = (f32[8,1280]{1,0:T(8,128)S(1)}, f32[8,1280]{1,0:T(8,128)}, u32[]{:S(2)}) copy-start(f32[8,1280]{1,0:T(8,128)} %param.8) | copy-start | bytes 122884
  18.7 6.0 %collective-permute-start.3 = (f32[2,16,1,1280]{3,1,2,0:T(8,128)S(1)}, f32[2,16,1,1280]{3,1,2,0:T(8,128)S(1)}, u32[]{:S(2)}, u32[]{:S(2)}) collective-permute-start(f32[2,16,1,1280]{3,1,2,0:T(8,128)S(1)} %copy.57), channel_id=1, source_target_pairs={{0,1},{1,2},{2,3},{4,5},{5,6},{6,7},{8,9},{9,10},{10,11},{12,13},{... | collective-permute-start | bytes 491528 | tf_op jit(solution)/shard_map/ppermute | solution.py:17
  26.5 7.4 %collective-permute-start.4 = (f32[2,16,1,1280]{3,1,2,0:T(8,128)S(1)}, f32[2,16,1,1280]{3,1,2,0:T(8,128)S(1)}, u32[]{:S(2)}, u32[]{:S(2)}) collective-permute-start(f32[2,16,1,1280]{3,1,2,0:T(8,128)S(1)} %copy.28), channel_id=1, source_target_pairs={{1,0},{2,1},{3,2},{5,4},{6,5},{7,6},{9,8},{10,9},{11,10},{13,12},{... | collective-permute-start | bytes 491528 | tf_op jit(solution)/shard_map/ppermute | solution.py:19
  28.5 6.6 %collective-permute-start.5 = (f32[2,16,1,1280]{3,1,2,0:T(8,128)S(1)}, f32[2,16,1,1280]{3,1,2,0:T(8,128)S(1)}, u32[]{:S(2)}, u32[]{:S(2)}) collective-permute-start(f32[2,16,1,1280]{3,1,2,0:T(8,128)S(1)} %copy.30), channel_id=1, source_target_pairs={{0,1},{1,2},{2,3},{4,5},{5,6},{6,7},{8,9},{9,10},{10,11},{12,13},{... | collective-permute-start | bytes 491528 | tf_op jit(solution)/shard_map/ppermute | solution.py:17
  37.0 7.4 %collective-permute-start.6 = (f32[2,16,1,1280]{3,1,2,0:T(8,128)S(1)}, f32[2,16,1,1280]{3,1,2,0:T(8,128)S(1)}, u32[]{:S(2)}, u32[]{:S(2)}) collective-permute-start(f32[2,16,1,1280]{3,1,2,0:T(8,128)S(1)} %copy.32), channel_id=1, source_target_pairs={{1,0},{2,1},{3,2},{5,4},{6,5},{7,6},{9,8},{10,9},{11,10},{13,12},{... | collective-permute-start | bytes 491528 | tf_op jit(solution)/shard_map/ppermute | solution.py:19
  38.9 6.6 %collective-permute-start.7 = (f32[2,16,1,1280]{3,1,2,0:T(8,128)S(1)}, f32[2,16,1,1280]{3,1,2,0:T(8,128)S(1)}, u32[]{:S(2)}, u32[]{:S(2)}) collective-permute-start(f32[2,16,1,1280]{3,1,2,0:T(8,128)S(1)} %copy.34), channel_id=1, source_target_pairs={{0,1},{1,2},{2,3},{4,5},{5,6},{6,7},{8,9},{9,10},{10,11},{12,13},{... | collective-permute-start | bytes 491528 | tf_op jit(solution)/shard_map/ppermute | solution.py:17
  47.4 7.4 %collective-permute-start.8 = (f32[2,16,1,1280]{3,1,2,0:T(8,128)S(1)}, f32[2,16,1,1280]{3,1,2,0:T(8,128)S(1)}, u32[]{:S(2)}, u32[]{:S(2)}) collective-permute-start(f32[2,16,1,1280]{3,1,2,0:T(8,128)S(1)} %copy.36), channel_id=1, source_target_pairs={{1,0},{2,1},{3,2},{5,4},{6,5},{7,6},{9,8},{10,9},{11,10},{13,12},{... | collective-permute-start | bytes 491528 | tf_op jit(solution)/shard_map/ppermute | solution.py:19
  49.4 6.6 %collective-permute-start.9 = (f32[2,16,1,1280]{3,1,2,0:T(8,128)S(1)}, f32[2,16,1,1280]{3,1,2,0:T(8,128)S(1)}, u32[]{:S(2)}, u32[]{:S(2)}) collective-permute-start(f32[2,16,1,1280]{3,1,2,0:T(8,128)S(1)} %copy.38), channel_id=1, source_target_pairs={{0,1},{1,2},{2,3},{4,5},{5,6},{6,7},{8,9},{9,10},{10,11},{12,13},{... | collective-permute-start | bytes 491528 | tf_op jit(solution)/shard_map/ppermute | solution.py:17
  60.1 172.1 %all-gather.3.cloned.1.call-start = ((), (), s32[]{:S(2)}) async-start(), calls=%async_computation | async-start | bytes 2949120 | tf_op jit(solution)/shard_map/all_gather | solution.py:64
  60.9 226.6 %all-gather.5.cloned.1.call-start = ((), (), s32[]{:S(2)}) async-start(), calls=%async_computation.2 | async-start | bytes 2949120 | tf_op jit(solution)/shard_map/all_gather | solution.py:65
  292.8 8.2 %collective-permute-start.10 = (f32[2,16,1,1280]{3,1,2,0:T(8,128)S(1)}, f32[2,16,1,1280]{3,1,2,0:T(8,128)S(1)}, u32[]{:S(2)}, u32[]{:S(2)}) collective-permute-start(f32[2,16,1,1280]{3,1,2,0:T(8,128)S(1)} %copy.40), channel_id=1, source_target_pairs={{1,0},{2,1},{3,2},{5,4},{6,5},{7,6},{9,8},{10,9},{11,10},{13,12},{... | collective-permute-start | bytes 491528 | tf_op jit(solution)/shard_map/ppermute | solution.py:19
  297.0 5.2 %collective-permute-start.11 = (f32[2,16,1,1280]{3,1,2,0:T(8,128)S(1)}, f32[2,16,1,1280]{3,1,2,0:T(8,128)S(1)}, u32[]{:S(2)}, u32[]{:S(2)}) collective-permute-start(f32[2,16,1,1280]{3,1,2,0:T(8,128)S(1)} %copy.42), channel_id=1, source_target_pairs={{0,1},{1,2},{2,3},{4,5},{5,6},{6,7},{8,9},{9,10},{10,11},{12,13},{... | collective-permute-start | bytes 491528 | tf_op jit(solution)/shard_map/ppermute | solution.py:17
  304.1 7.4 %collective-permute-start.12 = (f32[2,16,1,1280]{3,1,2,0:T(8,128)S(1)}, f32[2,16,1,1280]{3,1,2,0:T(8,128)S(1)}, u32[]{:S(2)}, u32[]{:S(2)}) collective-permute-start(f32[2,16,1,1280]{3,1,2,0:T(8,128)S(1)} %copy.44), channel_id=1, source_target_pairs={{1,0},{2,1},{3,2},{5,4},{6,5},{7,6},{9,8},{10,9},{11,10},{13,12},{... | collective-permute-start | bytes 491528 | tf_op jit(solution)/shard_map/ppermute | solution.py:19
  306.1 6.6 %collective-permute-start.13 = (f32[2,16,1,1280]{3,1,2,0:T(8,128)S(1)}, f32[2,16,1,1280]{3,1,2,0:T(8,128)S(1)}, u32[]{:S(2)}, u32[]{:S(2)}) collective-permute-start(f32[2,16,1,1280]{3,1,2,0:T(8,128)S(1)} %copy.46), channel_id=1, source_target_pairs={{0,1},{1,2},{2,3},{4,5},{5,6},{6,7},{8,9},{9,10},{10,11},{12,13},{... | collective-permute-start | bytes 491528 | tf_op jit(solution)/shard_map/ppermute | solution.py:17
  314.6 7.4 %collective-permute-start.14 = (f32[2,16,1,1280]{3,1,2,0:T(8,128)S(1)}, f32[2,16,1,1280]{3,1,2,0:T(8,128)S(1)}, u32[]{:S(2)}, u32[]{:S(2)}) collective-permute-start(f32[2,16,1,1280]{3,1,2,0:T(8,128)S(1)} %copy.48), channel_id=1, source_target_pairs={{1,0},{2,1},{3,2},{5,4},{6,5},{7,6},{9,8},{10,9},{11,10},{13,12},{... | collective-permute-start | bytes 491528 | tf_op jit(solution)/shard_map/ppermute | solution.py:19
  316.5 6.6 %collective-permute-start.15 = (f32[2,16,1,1280]{3,1,2,0:T(8,128)S(1)}, f32[2,16,1,1280]{3,1,2,0:T(8,128)S(1)}, u32[]{:S(2)}, u32[]{:S(2)}) collective-permute-start(f32[2,16,1,1280]{3,1,2,0:T(8,128)S(1)} %copy.50), channel_id=1, source_target_pairs={{0,1},{1,2},{2,3},{4,5},{5,6},{6,7},{8,9},{9,10},{10,11},{12,13},{... | collective-permute-start | bytes 491528 | tf_op jit(solution)/shard_map/ppermute | solution.py:17
  325.1 7.4 %collective-permute-start.16 = (f32[2,16,1,1280]{3,1,2,0:T(8,128)S(1)}, f32[2,16,1,1280]{3,1,2,0:T(8,128)S(1)}, u32[]{:S(2)}, u32[]{:S(2)}) collective-permute-start(f32[2,16,1,1280]{3,1,2,0:T(8,128)S(1)} %copy.52), channel_id=1, source_target_pairs={{1,0},{2,1},{3,2},{5,4},{6,5},{7,6},{9,8},{10,9},{11,10},{13,12},{... | collective-permute-start | bytes 491528 | tf_op jit(solution)/shard_map/ppermute | solution.py:19
  327.0 6.6 %collective-permute-start.17 = (f32[2,16,1,1280]{3,1,2,0:T(8,128)S(1)}, f32[2,16,1,1280]{3,1,2,0:T(8,128)S(1)}, u32[]{:S(2)}, u32[]{:S(2)}) collective-permute-start(f32[2,16,1,1280]{3,1,2,0:T(8,128)S(1)} %copy.54), channel_id=1, source_target_pairs={{0,1},{1,2},{2,3},{4,5},{5,6},{6,7},{8,9},{9,10},{10,11},{12,13},{... | collective-permute-start | bytes 491528 | tf_op jit(solution)/shard_map/ppermute | solution.py:17
  (2 other events, 5.8 us)
Sparse Core Ops, SparseCore 0:
  60.2 116.7 all-reduce.1
  179.2 52.9 all-gather.2
  234.4 52.9 all-gather.4
where the time goes:
time: 343 us
  waiting for transfers between devices  241 us (70%)
  starting transfers between devices  57.5 us (17%)
  other arithmetic  16.3 us (5%)
  between operations  14.4 us (4%)
  local copies, waits for them, and re-layouts  13.1 us (4%)
    psum x1, waiting for transfers between devices, body(): total = lax.psum(partial_sum, 'member')  115 us
    all_gather x1, waiting for transfers between devices, body(): lax.all_gather(innovation, 'member', axis=1, tiled=True)  55.2 us
    all_gather x1, waiting for transfers between devices, body(): lax.all_gather(obs_weight, 'member', axis=1, tiled=True)  55.2 us
    ppermute x9, starting transfers between devices, extended_2(): lax.ppermute(tail, axis, [(i, (i + 1) % count) for i in range(ends)])  37.6 us
    ppermute x9, starting transfers between devices, extended_2(): lax.ppermute(head, axis, [((i + 1) % count, i) for i in range(ends)])  19.5 us
    ppermute x9, waiting for transfers between devices, extended_2(): lax.ppermute(tail, axis, [(i, (i + 1) % count) for i in range(ends)])  8.39 us
  transfers between devices with their start and end apart: 21, of which 19 were waited for; matrix products, arithmetic and copies ran while one was open for 2% of the time, Pallas kernels for 0%

commit v1 on v0

--- a/solution.py
+++ b/solution.py
@@ -59,7 +59,7 @@
     sea = land.astype(jnp.float32)
     local = diffuse(alpha) * sea
     partial_sum = jnp.sum(perturb * local[None], axis=1)
-    total = lax.psum(partial_sum, "member")
+    total = jnp.sum(lax.all_gather(partial_sum, "member"), axis=0)
     weight_all, innov_all = (
         lax.all_gather(obs_weight, "member", axis=1, tiled=True),
         lax.all_gather(innovation, "member", axis=1, tiled=True),

time: 343 us -> 630 us (1.84)
  waiting for transfers between devices: 241 us -> 518 us
  other arithmetic: 16.3 us -> 25.9 us
    all_gather x0 -> x1, waiting for transfers between devices: none -> 402 us  [body(): total = jnp.sum(lax.all_gather(partial_sum, 'member'), axis=0)]
    psum x1 -> x0, waiting for transfers between devices: 115 us -> none  [body(): total = lax.psum(partial_sum, 'member')]
    all_gather x1, waiting for transfers between devices: 55.2 us -> 45.5 us  [body(): lax.all_gather(obs_weight, 'member', axis=1, tiled=True)]
    reduce_sum x0 -> x1, other arithmetic: none -> 9.65 us  [body(): total = jnp.sum(lax.all_gather(partial_sum, 'member'), axis=0)]
where the time goes in v1:
time: 630 us; the launch traced here: 629 us
  waiting for transfers between devices  518 us (82%)
  starting transfers between devices  57.5 us (9%)
  other arithmetic  25.9 us (4%)
  between operations  14.4 us (2%)
  local copies, waits for them, and re-layouts  12.9 us (2%)
    all_gather x1, waiting for transfers between devices, body(): total = jnp.sum(lax.all_gather(partial_sum, 'member'), axis=0)  402 us
    all_gather x1, waiting for transfers between devices, body(): lax.all_gather(innovation, 'member', axis=1, tiled=True)  55.2 us
    all_gather x1, waiting for transfers between devices, body(): lax.all_gather(obs_weight, 'member', axis=1, tiled=True)  45.5 us
    ppermute x9, starting transfers between devices, extended_2(): lax.ppermute(tail, axis, [(i, (i + 1) % count) for i in range(ends)])  37.6 us
    ppermute x9, starting transfers between devices, extended_2(): lax.ppermute(head, axis, [((i + 1) % count, i) for i in range(ends)])  19.5 us
  transfers between devices with their start and end apart: 21, of which 19 were waited for; matrix products, arithmetic and copies ran while one was open for 2% of the time, Pallas kernels for 0%

profile of v1, /device:TPU:1, one launch (start us, length us, event | category | flops | bytes accessed | tf_op | source)
XLA Modules:
  0.0 629.0 jit_solution(3636558020668795434)
XLA Ops:
  8.1 4.5 collective-permute-start
  12.6 1.9 collective-permute-start.1
  14.6 1.9 fusion.113
  16.5 1.9 collective-permute-start.2
  18.5 3.8 collective-permute-start.3
  26.4 1.9 collective-permute-start.4
  28.3 4.4 collective-permute-start.5
  36.8 1.9 collective-permute-start.6
  38.8 4.4 collective-permute-start.7
  47.3 1.9 collective-permute-start.8
  49.2 4.4 collective-permute-start.9
  57.8 2.1 fusion
  61.4 402.1 %all-gather.9.cloned.1.call-done = f32[32,16,8,1280]{3,2,1,0:T(8,128)} async-done(((f32[4,16,8,1280]{3,2,1,0:T(8,128)}), f32[32,16,8,1280]{3,2,1,0:T(8,128)}) %all-gather.9.cloned.1.call-update) | async-done | bytes 20971536 | tf_op jit(solution)/shard_map/all_gather | solution.py:62
  463.5 9.7 %reduce_sum.28 = f32[4,16,8,1280]{3,2,1,0:T(8,128)} reduce(f32[8,4,16,8,1280]{4,3,2,1,0:T(8,128)} %bitcast.1, f32[]{:T(128)} %constant.3.clone.1), dimensions={0}, to_apply=%region_1.2 | reduce | flops 4587520 | bytes 23592964 | tf_op jit(solution)/shard_map/reduce_sum | solution.py:62
  473.2 45.5 %all-gather.5.cloned.1.call-done = f32[4,16,8,1280]{3,2,1,0:T(8,128)} async-done(((f32[4,2,8,1280]{3,2,1,0:T(8,128)}), f32[4,16,8,1280]{3,2,1,0:T(8,128)}) %all-gather.5.cloned.1.call-update) | async-done | bytes 2621456 | tf_op jit(solution)/shard_map/all_gather | solution.py:64
  518.7 55.2 %all-gather.7.cloned.1.call-done = f32[4,16,8,1280]{3,2,1,0:T(8,128)} async-done(((f32[4,2,8,1280]{3,2,1,0:T(8,128)}), f32[4,16,8,1280]{3,2,1,0:T(8,128)}) %all-gather.7.cloned.1.call-update) | async-done | bytes 2621456 | tf_op jit(solution)/shard_map/all_gather | solution.py:65
  573.9 3.9 subtract_multiply_fusion
  579.3 4.2 collective-permute-start.10
  583.5 3.0 collective-permute-start.11
  590.6 1.9 collective-permute-start.12
  592.5 4.4 collective-permute-start.13
  603.0 4.4 collective-permute-start.15
  613.5 4.4 collective-permute-start.17
  620.3 2.2 fusion.5
  (107 shorter events, 38.6 us)
Async XLA Ops:
  7.2 15.1 %copy-start = (f32[2,16,8,1280]{3,2,1,0:T(8,128)S(1)}, f32[2,16,8,1280]{3,2,1,0:T(8,128)}, u32[]{:S(2)}) copy-start(f32[2,16,8,1280]{3,2,1,0:T(8,128)} %param.6) | copy-start | bytes 3932164
  7.2 456.3 %all-gather.9.cloned.1.call-start = ((), (), s32[]{:S(2)}) async-start(), calls=%async_computation.2 | async-start | bytes 23592960 | tf_op jit(solution)/shard_map/all_gather | solution.py:62
  8.1 14.7 %collective-permute-start = (f32[5,1280]{1,0:T(8,128)S(1)}, f32[5,1280]{1,0:T(8,128)S(1)}, u32[]{:S(2)}, u32[]{:S(2)}) collective-permute-start(f32[5,1280]{1,0:T(8,128)S(1)} %get-tuple-element.61), channel_id=1, source_target_pairs={{0,1},{1,2},{2,3},{4,5},{5,6},{6,7},{8,9},{9,10},{10,11},{12,13},{... | collective-permute-start | bytes 76808 | tf_op jit(solution)/shard_map/ppermute | solution.py:17
  12.6 10.2 %collective-permute-start.1 = (f32[5,1280]{1,0:T(8,128)S(1)}, f32[5,1280]{1,0:T(8,128)S(1)}, u32[]{:S(2)}, u32[]{:S(2)}) collective-permute-start(f32[5,1280]{1,0:T(8,128)S(1)} %get-tuple-element.62), channel_id=1, source_target_pairs={{1,0},{2,1},{3,2},{5,4},{6,5},{7,6},{9,8},{10,9},{11,10},{13,12},{... | collective-permute-start | bytes 76808 | tf_op jit(solution)/shard_map/ppermute | solution.py:19
  16.5 6.6 %collective-permute-start.2 = (f32[2,16,1,1280]{3,1,2,0:T(8,128)S(1)}, f32[2,16,1,1280]{3,1,2,0:T(8,128)S(1)}, u32[]{:S(2)}, u32[]{:S(2)}) collective-permute-start(f32[2,16,1,1280]{3,1,2,0:T(8,128)S(1)} %copy.56), channel_id=1, source_target_pairs={{1,0},{2,1},{3,2},{5,4},{6,5},{7,6},{9,8},{10,9},{11,10},{13,12},{... | collective-permute-start | bytes 491528 | tf_op jit(solution)/shard_map/ppermute | solution.py:19
  18.5 4.3 copy-start.4
  18.5 4.4 copy-start.3
  18.5 6.0 collective-permute-start.3
  26.4 7.4 %collective-permute-start.4 = (f32[2,16,1,1280]{3,1,2,0:T(8,128)S(1)}, f32[2,16,1,1280]{3,1,2,0:T(8,128)S(1)}, u32[]{:S(2)}, u32[]{:S(2)}) collective-permute-start(f32[2,16,1,1280]{3,1,2,0:T(8,128)S(1)} %copy.28), channel_id=1, source_target_pairs={{1,0},{2,1},{3,2},{5,4},{6,5},{7,6},{9,8},{10,9},{11,10},{13,12},{... | collective-permute-start | bytes 491528 | tf_op jit(solution)/shard_map/ppermute | solution.py:19
  28.3 6.6 %collective-permute-start.5 = (f32[2,16,1,1280]{3,1,2,0:T(8,128)S(1)}, f32[2,16,1,1280]{3,1,2,0:T(8,128)S(1)}, u32[]{:S(2)}, u32[]{:S(2)}) collective-permute-start(f32[2,16,1,1280]{3,1,2,0:T(8,128)S(1)} %copy.30), channel_id=1, source_target_pairs={{0,1},{1,2},{2,3},{4,5},{5,6},{6,7},{8,9},{9,10},{10,11},{12,13},{... | collective-permute-start | bytes 491528 | tf_op jit(solution)/shard_map/ppermute | solution.py:17
  36.8 7.4 %collective-permute-start.6 = (f32[2,16,1,1280]{3,1,2,0:T(8,128)S(1)}, f32[2,16,1,1280]{3,1,2,0:T(8,128)S(1)}, u32[]{:S(2)}, u32[]{:S(2)}) collective-permute-start(f32[2,16,1,1280]{3,1,2,0:T(8,128)S(1)} %copy.32), channel_id=1, source_target_pairs={{1,0},{2,1},{3,2},{5,4},{6,5},{7,6},{9,8},{10,9},{11,10},{13,12},{... | collective-permute-start | bytes 491528 | tf_op jit(solution)/shard_map/ppermute | solution.py:19
  38.8 6.6 %collective-permute-start.7 = (f32[2,16,1,1280]{3,1,2,0:T(8,128)S(1)}, f32[2,16,1,1280]{3,1,2,0:T(8,128)S(1)}, u32[]{:S(2)}, u32[]{:S(2)}) collective-permute-start(f32[2,16,1,1280]{3,1,2,0:T(8,128)S(1)} %copy.34), channel_id=1, source_target_pairs={{0,1},{1,2},{2,3},{4,5},{5,6},{6,7},{8,9},{9,10},{10,11},{12,13},{... | collective-permute-start | bytes 491528 | tf_op jit(solution)/shard_map/ppermute | solution.py:17
  47.3 7.4 %collective-permute-start.8 = (f32[2,16,1,1280]{3,1,2,0:T(8,128)S(1)}, f32[2,16,1,1280]{3,1,2,0:T(8,128)S(1)}, u32[]{:S(2)}, u32[]{:S(2)}) collective-permute-start(f32[2,16,1,1280]{3,1,2,0:T(8,128)S(1)} %copy.36), channel_id=1, source_target_pairs={{1,0},{2,1},{3,2},{5,4},{6,5},{7,6},{9,8},{10,9},{11,10},{13,12},{... | collective-permute-start | bytes 491528 | tf_op jit(solution)/shard_map/ppermute | solution.py:19
  49.2 6.6 %collective-permute-start.9 = (f32[2,16,1,1280]{3,1,2,0:T(8,128)S(1)}, f32[2,16,1,1280]{3,1,2,0:T(8,128)S(1)}, u32[]{:S(2)}, u32[]{:S(2)}) collective-permute-start(f32[2,16,1,1280]{3,1,2,0:T(8,128)S(1)} %copy.38), channel_id=1, source_target_pairs={{0,1},{1,2},{2,3},{4,5},{5,6},{6,7},{8,9},{9,10},{10,11},{12,13},{... | collective-permute-start | bytes 491528 | tf_op jit(solution)/shard_map/ppermute | solution.py:17
  59.9 458.8 %all-gather.5.cloned.1.call-start = ((), (), s32[]{:S(2)}) async-start(), calls=%async_computation | async-start | bytes 2949120 | tf_op jit(solution)/shard_map/all_gather | solution.py:64
  60.6 513.3 %all-gather.7.cloned.1.call-start = ((), (), s32[]{:S(2)}) async-start(), calls=%async_computation.1 | async-start | bytes 2949120 | tf_op jit(solution)/shard_map/all_gather | solution.py:65
  579.3 8.2 %collective-permute-start.10 = (f32[2,16,1,1280]{3,1,2,0:T(8,128)S(1)}, f32[2,16,1,1280]{3,1,2,0:T(8,128)S(1)}, u32[]{:S(2)}, u32[]{:S(2)}) collective-permute-start(f32[2,16,1,1280]{3,1,2,0:T(8,128)S(1)} %copy.40), channel_id=1, source_target_pairs={{1,0},{2,1},{3,2},{5,4},{6,5},{7,6},{9,8},{10,9},{11,10},{13,12},{... | collective-permute-start | bytes 491528 | tf_op jit(solution)/shard_map/ppermute | solution.py:19
  583.5 5.2 collective-permute-start.11
  590.6 7.4 %collective-permute-start.12 = (f32[2,16,1,1280]{3,1,2,0:T(8,128)S(1)}, f32[2,16,1,1280]{3,1,2,0:T(8,128)S(1)}, u32[]{:S(2)}, u32[]{:S(2)}) collective-permute-start(f32[2,16,1,1280]{3,1,2,0:T(8,128)S(1)} %copy.44), channel_id=1, source_target_pairs={{1,0},{2,1},{3,2},{5,4},{6,5},{7,6},{9,8},{10,9},{11,10},{13,12},{... | collective-permute-start | bytes 491528 | tf_op jit(solution)/shard_map/ppermute | solution.py:19
  592.5 6.6 %collective-permute-start.13 = (f32[2,16,1,1280]{3,1,2,0:T(8,128)S(1)}, f32[2,16,1,1280]{3,1,2,0:T(8,128)S(1)}, u32[]{:S(2)}, u32[]{:S(2)}) collective-permute-start(f32[2,16,1,1280]{3,1,2,0:T(8,128)S(1)} %copy.46), channel_id=1, source_target_pairs={{0,1},{1,2},{2,3},{4,5},{5,6},{6,7},{8,9},{9,10},{10,11},{12,13},{... | collective-permute-start | bytes 491528 | tf_op jit(solution)/shard_map/ppermute | solution.py:17
  601.0 7.4 %collective-permute-start.14 = (f32[2,16,1,1280]{3,1,2,0:T(8,128)S(1)}, f32[2,16,1,1280]{3,1,2,0:T(8,128)S(1)}, u32[]{:S(2)}, u32[]{:S(2)}) collective-permute-start(f32[2,16,1,1280]{3,1,2,0:T(8,128)S(1)} %copy.48), channel_id=1, source_target_pairs={{1,0},{2,1},{3,2},{5,4},{6,5},{7,6},{9,8},{10,9},{11,10},{13,12},{... | collective-permute-start | bytes 491528 | tf_op jit(solution)/shard_map/ppermute | solution.py:19
  603.0 6.6 %collective-permute-start.15 = (f32[2,16,1,1280]{3,1,2,0:T(8,128)S(1)}, f32[2,16,1,1280]{3,1,2,0:T(8,128)S(1)}, u32[]{:S(2)}, u32[]{:S(2)}) collective-permute-start(f32[2,16,1,1280]{3,1,2,0:T(8,128)S(1)} %copy.50), channel_id=1, source_target_pairs={{0,1},{1,2},{2,3},{4,5},{5,6},{6,7},{8,9},{9,10},{10,11},{12,13},{... | collective-permute-start | bytes 491528 | tf_op jit(solution)/shard_map/ppermute | solution.py:17
  611.5 7.4 %collective-permute-start.16 = (f32[2,16,1,1280]{3,1,2,0:T(8,128)S(1)}, f32[2,16,1,1280]{3,1,2,0:T(8,128)S(1)}, u32[]{:S(2)}, u32[]{:S(2)}) collective-permute-start(f32[2,16,1,1280]{3,1,2,0:T(8,128)S(1)} %copy.52), channel_id=1, source_target_pairs={{1,0},{2,1},{3,2},{5,4},{6,5},{7,6},{9,8},{10,9},{11,10},{13,12},{... | collective-permute-start | bytes 491528 | tf_op jit(solution)/shard_map/ppermute | solution.py:19
  613.5 6.6 %collective-permute-start.17 = (f32[2,16,1,1280]{3,1,2,0:T(8,128)S(1)}, f32[2,16,1,1280]{3,1,2,0:T(8,128)S(1)}, u32[]{:S(2)}, u32[]{:S(2)}) collective-permute-start(f32[2,16,1,1280]{3,1,2,0:T(8,128)S(1)} %copy.54), channel_id=1, source_target_pairs={{0,1},{1,2},{2,3},{4,5},{5,6},{6,7},{8,9},{9,10},{10,11},{12,13},{... | collective-permute-start | bytes 491528 | tf_op jit(solution)/shard_map/ppermute | solution.py:17
  (2 other events, 5.8 us)
Sparse Core Ops, SparseCore 0:
  60.0 403.4 all-gather.8
  465.7 52.9 all-gather.4
  520.9 52.9 all-gather.6
